TPU v7x, 32 devices: a whole 2x2x4 slice. The times are simulated.
32 devices in a mesh: size: 4 (over z), gz: 8 (over y, x, core).
Axes of the slice: x: 2, y: 2, z: 4, core: 2. Of those that a mesh axis runs over, the one named last changes fastest.
Arguments:
- tissue: int32 [256, 64, 128], P('gz'), may hold values from 0 to 2
- vessel_pressure: float32 [256, 64, 128], P('gz', 'size'), may hold values from -12 to 12
- cond_table: float32 [3], replicated, may hold values from 0.4 to 1.2
- leak_table: float32 [3], replicated, may hold values from 0.2 to 2
- bind_table: float32 [4, 3], P('size'), may hold values from 0.05 to 1
- hindrance: float32 [4], P('size'), may hold values from 0.2 to 1
- diffusivity: float32 [4], P('size'), may hold values from 0.1 to 0.6
- free_conc: float32 [4, 256, 64, 128], P('size', 'gz'), may hold values from 0 to 2
- bound_conc: float32 [4, 256, 64, 128], P('size', 'gz'), may hold values from 0 to 1
Outputs:
- pressure: float32 [256, 64, 128], P('gz', 'size')
- free_out: float32 [4, 256, 64, 128], P('size', 'gz')
- bound_out: float32 [4, 256, 64, 128], P('size', 'gz')
Inputs may be any that keep to these rules, and one draw needn't show every extreme that they name: 0 marks a vessel cell, 1 necrotic tissue, 2 viable tissue.
All inputs are finite; a program needn't handle non-finite values.
Results may differ from a plain program's by a relative error of at most 0.0001.
Values sent between devices are 32-bit elements; how exact they have to be, the bound alone decides.
No kernel may reach another device: no remote copies, remote signals or barrier semaphores. Data moves between devices by JAX's collectives and lax.ppermute only.
A program may use at most 128 MiB of HBM per device.

v0:
```python
import jax
import jax.numpy as jnp
from jax import lax
from jax.sharding import PartitionSpec as P

ITERS = 2
TSTEPS = 2
time_step = 0.1


def extended(cells, sides, width):
    for axis, dim in sides:
        count = lax.axis_size(axis)
        ends = count - 1
        head = lax.slice_in_dim(cells, 0, width, axis=dim)
        tail = lax.slice_in_dim(cells, cells.shape[dim] - width, cells.shape[dim], axis=dim)
        cells = jnp.concatenate(
            [
                lax.ppermute(tail, axis, [(i, (i + 1) % count) for i in range(ends)]),
                cells,
                lax.ppermute(head, axis, [((i + 1) % count, i) for i in range(ends)]),
            ],
            axis=dim,
        )
    return cells


def lookup(table, labels):
    return jnp.where(labels == 0, table[0], jnp.where(labels == 1, table[1], table[2]))


def neighbours(padded):
    total = padded[2:, 1:-1, 1:-1] + padded[:-2, 1:-1, 1:-1]
    total = total + padded[1:-1, 2:, 1:-1] + padded[1:-1, :-2, 1:-1]
    total = total + padded[1:-1, 1:-1, 2:] + padded[1:-1, 1:-1, :-2]
    return total


def apply_operator(vector, conduct, leak):
    scaled = conduct * vector
    rimmed = extended(scaled, (("size", 1), ("gz", 0)), 1)
    padded = jnp.pad(rimmed, ((0, 0), (0, 0), (1, 1)))
    return conduct * (6.0 * scaled - neighbours(padded)) + leak * vector


def paired_products(residual, precond, image):
    return lax.psum((jnp.sum(residual * precond), jnp.sum(precond * image)), ("size", "gz"))


def along_line(array, along_dim):
    return array[tuple((slice(None) if k == along_dim else slice(1, -1) for k in range(3)))]


def lower_part(array, along_dim):
    return array[tuple((slice(0, -1) if k == along_dim else slice(None) for k in range(3)))]


def upper_part(array, along_dim):
    return array[tuple((slice(1, None) if k == along_dim else slice(None) for k in range(3)))]


def transport_step(conc_pad, fields_pad, hinder, diffuse):
    divergence = None
    for along_dim in range(3):
        conc_line = along_line(conc_pad, along_dim)
        press_line = along_line(fields_pad[0], along_dim)
        cond_line = along_line(fields_pad[1], along_dim)
        conc_low = lower_part(conc_line, along_dim)
        conc_high = upper_part(conc_line, along_dim)
        velocity = (
            hinder
            * lower_part(cond_line, along_dim)
            * upper_part(cond_line, along_dim)
            * (lower_part(press_line, along_dim) - upper_part(press_line, along_dim))
        )
        flux = (
            jnp.maximum(velocity, 0.0) * conc_low
            + jnp.minimum(velocity, 0.0) * conc_high
            + diffuse * (conc_low - conc_high)
        )
        term = upper_part(flux, along_dim) - lower_part(flux, along_dim)
        divergence = term if divergence is None else divergence + term
    conc = conc_pad[1:-1, 1:-1, 1:-1]
    rate = fields_pad[2][1:-1, 1:-1, 1:-1]
    bind = rate * conc
    return (conc - time_step * (divergence + bind), bind)


def pad_plane(array):
    return jnp.pad(array, ((0, 0), (1, 1), (1, 1)))


def local(
    tissue,
    vessel_pressure,
    cond_table,
    leak_table,
    bind_table,
    hindrance,
    diffusivity,
    free_conc,
    bound_conc,
):
    block_x = vessel_pressure.shape[1]
    slab_z = vessel_pressure.shape[0]
    local_tissue = lax.dynamic_slice_in_dim(tissue, lax.axis_index("size") * block_x, block_x, 1)
    conduct = lookup(cond_table, local_tissue)
    leak = lookup(leak_table, local_tissue)
    diag = 6.0 * conduct * conduct + leak
    source = leak * vessel_pressure
    solution = jnp.zeros_like(source)
    residual = source
    precond = residual / diag
    image = apply_operator(precond, conduct, leak)
    rho_now, product = paired_products(residual, precond, image)
    alpha = rho_now / product
    direction = precond
    along_image = image
    for iteration in range(ITERS):
        solution = solution + alpha * direction
        residual = residual - alpha * along_image
        if iteration + 1 < ITERS:
            precond = residual / diag
            image = apply_operator(precond, conduct, leak)
            rho_next, product = paired_products(residual, precond, image)
            ratio = rho_next / rho_now
            alpha = rho_next / (product - ratio * rho_next / alpha)
            direction = precond + ratio * direction
            along_image = image + ratio * along_image
            rho_now = rho_next
    conduct_slab = lookup(cond_table, tissue)
    rate_slab = lookup(bind_table[0], tissue)
    slab_pressure = lax.all_gather(solution, "size", axis=1, tiled=True)
    stacked = jnp.stack([slab_pressure, conduct_slab, rate_slab])
    rimmed = extended(stacked, (("gz", 1),), TSTEPS)
    fields_pad = jnp.pad(rimmed, ((0, 0), (0, 0), (1, 1), (1, 1)))
    hinder = hindrance[0]
    diffuse = diffusivity[0]
    conc = free_conc[0]
    bound = bound_conc[0]
    fields_one = fields_pad[:, TSTEPS - 1 : TSTEPS + 1 + slab_z]
    for sweep in range(TSTEPS):
        conc_pad = pad_plane(extended(conc, (("gz", 0),), 1))
        conc, bind = transport_step(conc_pad, fields_one, hinder, diffuse)
        bound = bound + time_step * bind
    return (solution, conc[None], bound[None])


def solution(mesh):
    return jax.shard_map(
        local,
        mesh=mesh,
        in_specs=(
            P("gz", None, None),
            P("gz", "size", None),
            P(),
            P(),
            P("size", None),
            P("size"),
            P("size"),
            P("size", "gz", None, None),
            P("size", "gz", None, None),
        ),
        out_specs=(P("gz", "size", None), P("size", "gz", None, None), P("size", "gz", None, None)),
        check_vma=False,
    )
```

profile of v0, /device:TPU:4, one launch (start us, length us, event | category | flops | bytes accessed | tf_op | source)
XLA Modules:
  0.0 228.2 jit_solution(11120340233154857061)
XLA Ops:
  7.2 1.3 fusion.53
  8.6 1.4 fusion.52
  10.0 4.9 %fusion.39 = (f32[32,16,128]{2,1,0:T(8,128)S(1)}, pred[32,16,128]{2,1,0:T(8,128)(4,1)S(1)}, pred[32,16,128]{2,1,0:T(8,128)(4,1)S(1)}) fusion(f32[]{:T(128)} %bitcast.5, f32[]{:T(128)} %bitcast.4, f32[]{:T(128)} %bitcast.3, f32[32,16,128]{2,1,0:T(8,128)} %param.10, f32[]{:T(128)} %bitcast.2, f32[]{:T(128)} %bitcast.1, f32[]{:T(128)} %bitcast, ...), kind=kLoop, calls=%fused_computation.127 | loop fusion | flops 786432 | bytes 917532 | tf_op jit(solution)/shard_map/mul | solution.py:40
  15.0 1.3 collective-permute-start.1
  16.3 4.5 %collective-permute-start = (f32[32,1,128]{2,1,0:T(1,128)S(1)}, f32[32,1,128]{2,1,0:T(1,128)S(1)}, u32[]{:S(2)}, u32[]{:S(2)}) collective-permute-start(f32[32,1,128]{2,1,0:T(1,128)S(1)} %get-tuple-element.41), channel_id=1, source_target_pairs={{0,8},{8,16},{16,24},{1,9},{9,17},{17,25},{2,10},{10,18},{18,26},{... | collective-permute-start | bytes 49160 | tf_op jit(solution)/shard_map/ppermute | solution.py:19
  20.8 1.4 collective-permute-done
  22.2 1.9 collective-permute-start.2
  24.2 2.4 %collective-permute-start.3 = (f32[1,18,128]{2,1,0:T(8,128)S(1)}, f32[1,18,128]{2,1,0:T(8,128)S(1)}, u32[]{:S(2)}, u32[]{:S(2)}) collective-permute-start(f32[1,18,128]{2,1,0:T(8,128)S(1)} %get-tuple-element.37), channel_id=1, source_target_pairs={{0,1},{1,2},{2,3},{3,4},{4,5},{5,6},{6,7},{8,9},{9,10},{10,11},{11... | collective-permute-start | bytes 27656 | tf_op jit(solution)/shard_map/ppermute | solution.py:19
  26.6 3.5 %collective-permute-done.3 = f32[1,18,128]{2,1,0:T(8,128)S(1)} collective-permute-done((f32[1,18,128]{2,1,0:T(8,128)S(1)}, f32[1,18,128]{2,1,0:T(8,128)S(1)}, u32[]{:S(2)}, u32[]{:S(2)}) %collective-permute-start.3) | collective-permute-done | bytes 9248 | tf_op jit(solution)/shard_map/ppermute | solution.py:19
  30.1 0.4 select_maximum_fusion.12
  30.5 4.7 %multiply_reduce_fusion.1 = (f32[]{:T(128)}, f32[]{:T(128)}, f32[32,16,128]{2,1,0:T(8,128)S(1)}) fusion(pred[32,16,128]{2,1,0:T(8,128)(4,1)S(1)} %get-tuple-element.23, pred[32,16,128]{2,1,0:T(8,128)(4,1)S(1)} %get-tuple-element.22, f32[]{:T(128)} %bitcast.5, f32[]{:T(128)} %bitcast.4, f32[]{:T(128)} %bitcast.3, f32[32,16,128]{2,1,0:T(8,128)S(1)} %copy-done.1, ...), kind=kLoop, calls=%fused_computation.123 | loop fusion | flops 2031614 | bytes 1493024 | tf_op jit(solution)/shard_map/reduce_sum | solution.py:47
  35.3 41.6 %all-reduce.6 = (f32[]{:T(128)}, f32[]{:T(128)}) all-reduce(f32[]{:T(128)} %get-tuple-element.4, f32[]{:T(128)} %get-tuple-element.3), channel_id=1, replica_groups=mesh['size'=4,'gz'=8] {'size','gz'}, use_global_device_ids=true, to_apply=%region_1.2 | all-reduce | flops 2 | bytes 16 | tf_op jit(solution)/shard_map/psum | solution.py:47
  78.1 4.5 %fusion.38 = (f32[32,16,128]{2,1,0:T(8,128)S(1)}, f32[]{:T(128)}) fusion(pred[32,16,128]{2,1,0:T(8,128)(4,1)S(1)} %get-tuple-element.23, pred[32,16,128]{2,1,0:T(8,128)(4,1)S(1)} %get-tuple-element.22, f32[]{:T(128)} %bitcast.5, f32[]{:T(128)} %bitcast.4, f32[]{:T(128)} %bitcast.3, f32[32,16,128]{2,1,0:T(8,128)S(1)} %get-tuple-element.20, f32[]{:T(128)S(6)} %div.19, ...), kind=kLoop, calls=%fused_computation.126 | loop fusion | flops 917503 | bytes 917536 | tf_op jit(solution)/shard_map/mul | solution.py:40
  82.7 1.4 collective-permute-start.5
  84.2 4.7 %collective-permute-start.4 = (f32[32,1,128]{2,1,0:T(1,128)S(1)}, f32[32,1,128]{2,1,0:T(1,128)S(1)}, u32[]{:S(2)}, u32[]{:S(2)}) collective-permute-start(f32[32,1,128]{2,1,0:T(1,128)S(1)} %get-tuple-element.39), channel_id=1, source_target_pairs={{0,8},{8,16},{16,24},{1,9},{9,17},{17,25},{2,10},{10,18},{18,26},{... | collective-permute-start | bytes 49160 | tf_op jit(solution)/shard_map/ppermute | solution.py:19
  88.8 1.4 collective-permute-done.4
  90.3 1.9 collective-permute-start.6
  92.2 2.4 %collective-permute-start.7 = (f32[1,18,128]{2,1,0:T(8,128)S(1)}, f32[1,18,128]{2,1,0:T(8,128)S(1)}, u32[]{:S(2)}, u32[]{:S(2)}) collective-permute-start(f32[1,18,128]{2,1,0:T(8,128)S(1)} %get-tuple-element.35), channel_id=1, source_target_pairs={{0,1},{1,2},{2,3},{3,4},{4,5},{5,6},{6,7},{8,9},{9,10},{10,11},{11... | collective-permute-start | bytes 27656 | tf_op jit(solution)/shard_map/ppermute | solution.py:19
  94.6 3.5 %collective-permute-done.7 = f32[1,18,128]{2,1,0:T(8,128)S(1)} collective-permute-done((f32[1,18,128]{2,1,0:T(8,128)S(1)}, f32[1,18,128]{2,1,0:T(8,128)S(1)}, u32[]{:S(2)}, u32[]{:S(2)}) %collective-permute-start.7) | collective-permute-done | bytes 9248 | tf_op jit(solution)/shard_map/ppermute | solution.py:19
  98.1 0.4 select_maximum_fusion.8
  98.5 4.8 %fusion.28 = f32[]{:T(128)} fusion(f32[34,18,130]{2,1,0:T(8,128)S(1)} %select_maximum_fusion.8, f32[32,16,128]{2,1,0:T(8,128)S(1)} %get-tuple-element.33, f32[32,1,128]{2,1,0:T(1,128)S(1)} %collective-permute-done.4, f32[32,1,128]{2,1,0:T(1,128)S(1)} %collective-permute-done.5, f32[1,18,128]{2,1,0:T(8,128)S(1)} %collective-permute-done.7, ...), kind=kLoop, calls=%fused_computation.91 | loop fusion | flops 2031615 | bytes 1493024 | tf_op jit(solution)/shard_map/reduce_sum | solution.py:47
  103.3 41.4 %all-reduce.5 = (f32[]{:T(128)}, f32[]{:T(128)}) all-reduce(f32[]{:T(128)} %get-tuple-element.34, f32[]{:T(128)} %fusion.28), channel_id=1, replica_groups=mesh['size'=4,'gz'=8] {'size','gz'}, use_global_device_ids=true, to_apply=%region_5.6 | all-reduce | flops 2 | bytes 16 | tf_op jit(solution)/shard_map/psum | solution.py:47
  149.1 4.6 %multiply_add_fusion.6 = f32[32,16,128]{2,1,0:T(8,128)} fusion(f32[]{:T(128)S(6)} %div.21, f32[]{:T(128)S(6)} %div.23, f32[]{:T(128)S(6)} %div.19, pred[32,16,128]{2,1,0:T(8,128)(4,1)S(1)} %get-tuple-element.23, pred[32,16,128]{2,1,0:T(8,128)(4,1)S(1)} %get-tuple-element.22, f32[]{:T(128)} %bitcast.5, f32[]{:T(128)} %bitcast.4, f32[]{:T(128)} %bitcast.3, ...), kind=kLoop, calls=%fused_computation.120 | loop fusion | flops 1114112 | bytes 917540 | tf_op jit(solution)/shard_map/add | solution.py:120
  153.7 2.0 collective-permute-start.11
  155.7 2.3 %collective-permute-start.10 = (f32[1,64,128]{2,1,0:T(8,128)S(1)}, f32[1,64,128]{2,1,0:T(8,128)S(1)}, u32[]{:S(2)}, u32[]{:S(2)}) collective-permute-start(f32[1,64,128]{2,1,0:T(8,128)S(1)} %get-tuple-element.31), channel_id=1, source_target_pairs={{0,1},{1,2},{2,3},{3,4},{4,5},{5,6},{6,7},{8,9},{9,10},{10,11},{11... | collective-permute-start | bytes 98312 | tf_op jit(solution)/shard_map/ppermute | solution.py:19
  159.4 0.6 fusion.51
  160.0 2.2 select_bitcast_fusion.1
  162.2 2.0 select_bitcast_fusion
  164.3 17.5 %all-gather.2.cloned.1.call-done = f32[32,64,128]{2,1,0:T(8,128)} async-done(((f32[32,16,128]{2,1,0:T(8,128)}), f32[32,64,128]{2,1,0:T(8,128)}) %all-gather.2.cloned.1.call-update) | async-done | bytes 1048592 | tf_op jit(solution)/shard_map/all_gather | solution.py:133
  181.7 0.9 pad_maximum_fusion.22
  182.7 2.4 %collective-permute-start.9 = (f32[3,2,64,128]{3,2,1,0:T(8,128)S(1)}, f32[3,2,64,128]{3,2,1,0:T(8,128)S(1)}, u32[]{:S(2)}, u32[]{:S(2)}) collective-permute-start(f32[3,2,64,128]{3,2,1,0:T(8,128)S(1)} %get-tuple-element.28), channel_id=1, source_target_pairs={{1,0},{2,1},{3,2},{4,3},{5,4},{6,5},{7,6},{9,8},{10,9},{11,10},{12... | collective-permute-start | bytes 589832 | tf_op jit(solution)/shard_map/ppermute | solution.py:21
  185.1 2.2 collective-permute-start.8
  187.3 0.7 select_maximum_fusion.6
  188.2 4.7 %collective-permute-done.8 = f32[3,2,64,128]{3,2,1,0:T(8,128)S(1)} collective-permute-done((f32[3,2,64,128]{3,2,1,0:T(8,128)S(1)}, f32[3,2,64,128]{3,2,1,0:T(8,128)S(1)}, u32[]{:S(2)}, u32[]{:S(2)}) %collective-permute-start.8) | collective-permute-done | bytes 196640 | tf_op jit(solution)/shard_map/ppermute | solution.py:19
  193.0 7.3 %select_maximum_fusion = f32[3,36,66,130]{3,2,1,0:T(8,128)S(1)} fusion(f32[3,2,64,128]{3,2,1,0:T(8,128)S(1)} %collective-permute-done.9, f32[3,2,64,128]{3,2,1,0:T(8,128)S(1)} %collective-permute-done.8, f32[1,32,64,128]{3,2,1,0:T(8,128)S(1)} %select_bitcast_fusion, f32[1,32,64,128]{3,2,1,0:T(8,128)S(1)} %get-tuple-element.17, f32[1,32,64,128]{3,2,1,0:T(8,128)S(1)} %bitcast.52), kind=kLoop, calls=%fused_computation.4 | loop fusion | flops 19459440 | bytes 7245504 | tf_op jit(solution)/shard_map/concatenate | solution.py:17
  200.2 0.7 slice_bitcast_fusion.2
  200.9 2.4 %multiply_add_fusion.1 = (f32[32,64,129]{2,1,0:T(8,128)S(1)}, f32[32,64,129]{2,1,0:T(8,128)S(1)}) fusion(f32[34,66,130]{2,1,0:T(8,128)S(1)} %select_maximum_fusion.6, f32[]{:T(128)} %bitcast.45, f32[34,66,130]{2,1,0:T(8,128)S(1)} %get-tuple-element.25, f32[34,66,130]{2,1,0:T(8,128)S(1)} %get-tuple-element.24, f32[]{:T(128)} %bitcast.42), kind=kLoop, calls=%fused_computation.30 | loop fusion | flops 3170304 | bytes 8454152 | tf_op jit(solution)/shard_map/add | solution.py:77
  203.3 1.9 multiply_add_fusion.3
  205.2 1.2 multiply_add_fusion.5
  206.5 2.1 fusion.21
  208.5 1.9 collective-permute-start.13
  210.4 2.6 %collective-permute-start.12 = (f32[1,64,128]{2,1,0:T(8,128)S(1)}, f32[1,64,128]{2,1,0:T(8,128)S(1)}, u32[]{:S(2)}, u32[]{:S(2)}) collective-permute-start(f32[1,64,128]{2,1,0:T(8,128)S(1)} %get-tuple-element.29), channel_id=1, source_target_pairs={{0,1},{1,2},{2,3},{3,4},{4,5},{5,6},{6,7},{8,9},{9,10},{10,11},{11... | collective-permute-start | bytes 98312 | tf_op jit(solution)/shard_map/ppermute | solution.py:19
  213.1 3.5 %collective-permute-done.12 = f32[1,64,128]{2,1,0:T(8,128)S(1)} collective-permute-done((f32[1,64,128]{2,1,0:T(8,128)S(1)}, f32[1,64,128]{2,1,0:T(8,128)S(1)}, u32[]{:S(2)}, u32[]{:S(2)}) %collective-permute-start.12) | collective-permute-done | bytes 32800 | tf_op jit(solution)/shard_map/ppermute | solution.py:19
  216.6 0.7 select_maximum_fusion.4
  217.3 1.2 multiply_add_fusion
  218.5 0.7 multiply_add_fusion.2
  219.2 0.3 multiply_add_fusion.4
  219.5 1.9 fusion.13
  (36 shorter events, 0.4 us)
Async XLA Ops:
  7.2 23.3 %copy-start.1 = (f32[32,16,128]{2,1,0:T(8,128)S(1)}, f32[32,16,128]{2,1,0:T(8,128)}, u32[]{:S(2)}) copy-start(f32[32,16,128]{2,1,0:T(8,128)} %param.10) | copy-start | bytes 786436
  7.2 174.6 %all-gather.2.cloned.1.call-start = ((), (), s32[]{:S(2)}) async-start(), calls=%async_computation | async-start | bytes 1310720 | tf_op jit(solution)/shard_map/all_gather | solution.py:133
  15.0 5.9 %collective-permute-start.1 = (f32[32,1,128]{2,1,0:T(1,128)S(1)}, f32[32,1,128]{2,1,0:T(1,128)S(1)}, u32[]{:S(2)}, u32[]{:S(2)}) collective-permute-start(f32[32,1,128]{2,1,0:T(1,128)S(1)} %get-tuple-element.42), channel_id=1, source_target_pairs={{8,0},{16,8},{24,16},{9,1},{17,9},{25,17},{10,2},{18,10},{26,18},{... | collective-permute-start | bytes 49160 | tf_op jit(solution)/shard_map/ppermute | solution.py:21
  16.3 6.0 %collective-permute-start = (f32[32,1,128]{2,1,0:T(1,128)S(1)}, f32[32,1,128]{2,1,0:T(1,128)S(1)}, u32[]{:S(2)}, u32[]{:S(2)}) collective-permute-start(f32[32,1,128]{2,1,0:T(1,128)S(1)} %get-tuple-element.41), channel_id=1, source_target_pairs={{0,8},{8,16},{16,24},{1,9},{9,17},{17,25},{2,10},{10,18},{18,26},{... | collective-permute-start | bytes 49160 | tf_op jit(solution)/shard_map/ppermute | solution.py:19
  22.2 4.3 %collective-permute-start.2 = (f32[1,18,128]{2,1,0:T(8,128)S(1)}, f32[1,18,128]{2,1,0:T(8,128)S(1)}, u32[]{:S(2)}, u32[]{:S(2)}) collective-permute-start(f32[1,18,128]{2,1,0:T(8,128)S(1)} %get-tuple-element.38), channel_id=1, source_target_pairs={{1,0},{2,1},{3,2},{4,3},{5,4},{6,5},{7,6},{9,8},{10,9},{11,10},{12... | collective-permute-start | bytes 27656 | tf_op jit(solution)/shard_map/ppermute | solution.py:21
  24.2 5.9 %collective-permute-start.3 = (f32[1,18,128]{2,1,0:T(8,128)S(1)}, f32[1,18,128]{2,1,0:T(8,128)S(1)}, u32[]{:S(2)}, u32[]{:S(2)}) collective-permute-start(f32[1,18,128]{2,1,0:T(8,128)S(1)} %get-tuple-element.37), channel_id=1, source_target_pairs={{0,1},{1,2},{2,3},{3,4},{4,5},{5,6},{6,7},{8,9},{9,10},{10,11},{11... | collective-permute-start | bytes 27656 | tf_op jit(solution)/shard_map/ppermute | solution.py:19
  82.7 71.0 %copy-start = (f32[1,32,64,128]{3,2,1,0:T(8,128)S(1)}, f32[1,32,64,128]{3,2,1,0:T(8,128)}, u32[]{:S(2)}) copy-start(f32[1,32,64,128]{3,2,1,0:T(8,128)} %param.16) | copy-start | bytes 3145732
  82.7 6.1 %collective-permute-start.5 = (f32[32,1,128]{2,1,0:T(1,128)S(1)}, f32[32,1,128]{2,1,0:T(1,128)S(1)}, u32[]{:S(2)}, u32[]{:S(2)}) collective-permute-start(f32[32,1,128]{2,1,0:T(1,128)S(1)} %get-tuple-element.40), channel_id=1, source_target_pairs={{8,0},{16,8},{24,16},{9,1},{17,9},{25,17},{10,2},{18,10},{26,18},{... | collective-permute-start | bytes 49160 | tf_op jit(solution)/shard_map/ppermute | solution.py:21
  84.1 75.2 %copy-start.9 = (f32[1,3]{1,0:T(1,128)S(1)}, f32[1,3]{1,0:T(1,128)}, u32[]{:S(2)}) copy-start(f32[1,3]{1,0:T(1,128)} %param.13) | copy-start | bytes 40
  84.1 75.9 %copy-start.3 = (s32[32,64,128]{2,1,0:T(8,128)S(1)}, s32[32,64,128]{2,1,0:T(8,128)}, u32[]{:S(2)}) copy-start(s32[32,64,128]{2,1,0:T(8,128)} %param.9) | copy-start | bytes 3145732
  84.2 6.1 %collective-permute-start.4 = (f32[32,1,128]{2,1,0:T(1,128)S(1)}, f32[32,1,128]{2,1,0:T(1,128)S(1)}, u32[]{:S(2)}, u32[]{:S(2)}) collective-permute-start(f32[32,1,128]{2,1,0:T(1,128)S(1)} %get-tuple-element.39), channel_id=1, source_target_pairs={{0,8},{8,16},{16,24},{1,9},{9,17},{17,25},{2,10},{10,18},{18,26},{... | collective-permute-start | bytes 49160 | tf_op jit(solution)/shard_map/ppermute | solution.py:19
  90.3 4.3 %collective-permute-start.6 = (f32[1,18,128]{2,1,0:T(8,128)S(1)}, f32[1,18,128]{2,1,0:T(8,128)S(1)}, u32[]{:S(2)}, u32[]{:S(2)}) collective-permute-start(f32[1,18,128]{2,1,0:T(8,128)S(1)} %get-tuple-element.36), channel_id=1, source_target_pairs={{1,0},{2,1},{3,2},{4,3},{5,4},{6,5},{7,6},{9,8},{10,9},{11,10},{12... | collective-permute-start | bytes 27656 | tf_op jit(solution)/shard_map/ppermute | solution.py:21
  92.2 5.9 %collective-permute-start.7 = (f32[1,18,128]{2,1,0:T(8,128)S(1)}, f32[1,18,128]{2,1,0:T(8,128)S(1)}, u32[]{:S(2)}, u32[]{:S(2)}) collective-permute-start(f32[1,18,128]{2,1,0:T(8,128)S(1)} %get-tuple-element.35), channel_id=1, source_target_pairs={{0,1},{1,2},{2,3},{3,4},{4,5},{5,6},{6,7},{8,9},{9,10},{10,11},{11... | collective-permute-start | bytes 27656 | tf_op jit(solution)/shard_map/ppermute | solution.py:19
  153.7 33.6 %collective-permute-start.11 = (f32[1,64,128]{2,1,0:T(8,128)S(1)}, f32[1,64,128]{2,1,0:T(8,128)S(1)}, u32[]{:S(2)}, u32[]{:S(2)}) collective-permute-start(f32[1,64,128]{2,1,0:T(8,128)S(1)} %get-tuple-element.32), channel_id=1, source_target_pairs={{1,0},{2,1},{3,2},{4,3},{5,4},{6,5},{7,6},{9,8},{10,9},{11,10},{12... | collective-permute-start | bytes 98312 | tf_op jit(solution)/shard_map/ppermute | solution.py:21
  155.7 31.6 %collective-permute-start.10 = (f32[1,64,128]{2,1,0:T(8,128)S(1)}, f32[1,64,128]{2,1,0:T(8,128)S(1)}, u32[]{:S(2)}, u32[]{:S(2)}) collective-permute-start(f32[1,64,128]{2,1,0:T(8,128)S(1)} %get-tuple-element.31), channel_id=1, source_target_pairs={{0,1},{1,2},{2,3},{3,4},{4,5},{5,6},{6,7},{8,9},{9,10},{10,11},{11... | collective-permute-start | bytes 98312 | tf_op jit(solution)/shard_map/ppermute | solution.py:19
  182.6 10.3 %copy-start.2 = (f32[32,64,128]{2,1,0:T(8,128)S(1)}, f32[32,64,128]{2,1,0:T(8,128)}, u32[]{:S(2)}) copy-start(f32[32,64,128]{2,1,0:T(8,128)} %all-gather.2.cloned.1.call-done) | copy-start | bytes 3145732
  182.7 5.6 %collective-permute-start.9 = (f32[3,2,64,128]{3,2,1,0:T(8,128)S(1)}, f32[3,2,64,128]{3,2,1,0:T(8,128)S(1)}, u32[]{:S(2)}, u32[]{:S(2)}) collective-permute-start(f32[3,2,64,128]{3,2,1,0:T(8,128)S(1)} %get-tuple-element.28), channel_id=1, source_target_pairs={{1,0},{2,1},{3,2},{4,3},{5,4},{6,5},{7,6},{9,8},{10,9},{11,10},{12... | collective-permute-start | bytes 589832 | tf_op jit(solution)/shard_map/ppermute | solution.py:21
  185.1 7.9 %collective-permute-start.8 = (f32[3,2,64,128]{3,2,1,0:T(8,128)S(1)}, f32[3,2,64,128]{3,2,1,0:T(8,128)S(1)}, u32[]{:S(2)}, u32[]{:S(2)}) collective-permute-start(f32[3,2,64,128]{3,2,1,0:T(8,128)S(1)} %get-tuple-element.27), channel_id=1, source_target_pairs={{0,1},{1,2},{2,3},{3,4},{4,5},{5,6},{6,7},{8,9},{9,10},{10,11},{11... | collective-permute-start | bytes 589832 | tf_op jit(solution)/shard_map/ppermute | solution.py:19
  187.3 5.6 %copy-start.5 = (f32[1,64,128]{2,1,0:T(8,128)}, f32[1,64,128]{2,1,0:T(8,128)S(1)}, u32[]{:S(2)}) copy-start(f32[1,64,128]{2,1,0:T(8,128)S(1)} %collective-permute-done.11) | copy-start | bytes 98308
  187.3 5.6 %copy-start.7 = (f32[1,64,128]{2,1,0:T(8,128)}, f32[1,64,128]{2,1,0:T(8,128)S(1)}, u32[]{:S(2)}) copy-start(f32[1,64,128]{2,1,0:T(8,128)S(1)} %collective-permute-done.10) | copy-start | bytes 98308
  203.3 1.9 copy-start.6
  203.3 1.9 copy-start.8
  205.2 1.2 copy-start.4
  208.5 4.6 %collective-permute-start.13 = (f32[1,64,128]{2,1,0:T(8,128)S(1)}, f32[1,64,128]{2,1,0:T(8,128)S(1)}, u32[]{:S(2)}, u32[]{:S(2)}) collective-permute-start(f32[1,64,128]{2,1,0:T(8,128)S(1)} %get-tuple-element.30), channel_id=1, source_target_pairs={{1,0},{2,1},{3,2},{4,3},{5,4},{6,5},{7,6},{9,8},{10,9},{11,10},{12... | collective-permute-start | bytes 98312 | tf_op jit(solution)/shard_map/ppermute | solution.py:21
  210.4 6.1 %collective-permute-start.12 = (f32[1,64,128]{2,1,0:T(8,128)S(1)}, f32[1,64,128]{2,1,0:T(8,128)S(1)}, u32[]{:S(2)}, u32[]{:S(2)}) collective-permute-start(f32[1,64,128]{2,1,0:T(8,128)S(1)} %get-tuple-element.29), channel_id=1, source_target_pairs={{0,1},{1,2},{2,3},{3,4},{4,5},{5,6},{6,7},{8,9},{9,10},{10,11},{11... | collective-permute-start | bytes 98312 | tf_op jit(solution)/shard_map/ppermute | solution.py:19
Sparse Core Ops, SparseCore 0:
  153.8 27.8 all-gather.1
where the time goes:
time: 229 us; the launch traced here: 228 us
  blocking collectives  83 us (36%)
  other arithmetic  49.8 us (22%)
  waiting for transfers between devices  35.7 us (16%)
  starting transfers between devices  34.1 us (15%)
  between operations  21.4 us (9%)
  local copies, waits for them, and re-layouts  4.21 us (2%)
    psum x2, blocking collectives, paired_products(): lax.psum((jnp.sum(residual * precond), jnp.sum(precond * image)), ('size'...  83 us
    ppermute x7, starting transfers between devices, extended(): lax.ppermute(tail, axis, [(i, (i + 1) % count) for i in range(ends)])  21.2 us
    ppermute x7, waiting for transfers between devices, extended(): lax.ppermute(tail, axis, [(i, (i + 1) % count) for i in range(ends)])  18 us
    all_gather x1, waiting for transfers between devices, local(): slab_pressure = lax.all_gather(solution, 'size', axis=1, tiled=True)  17.5 us
    ppermute x7, starting transfers between devices, extended(): lax.ppermute(head, axis, [((i + 1) % count, i) for i in range(ends)])  12.8 us
    concatenate x7, other arithmetic, extended(): jnp.concatenate([lax.ppermute(tail, axis, [(i, (i + 1) % count) for i in...  9.57 us
    reduce_sum x2, other arithmetic, paired_products(): jnp.sum(precond * image)  9.51 us
    mul x2, other arithmetic, apply_operator(): scaled = conduct * vector  9.43 us
  transfers between devices with their start and end apart: 15, of which 8 were waited for; matrix products, arithmetic and copies ran while one was open for 3% of the time, Pallas kernels for 0%

commit v1 on v0

--- a/solution.py
+++ b/solution.py
@@ -44,7 +44,7 @@
 
 
 def paired_products(residual, precond, image):
-    return lax.psum((jnp.sum(residual * precond), jnp.sum(precond * image)), ("size", "gz"))
+    return lax.psum(lax.psum((jnp.sum(residual * precond), jnp.sum(precond * image)), "gz"), "size")
 
 
 def along_line(array, along_dim):

time: 229 us -> 194 us (0.85)
  blocking collectives: 83 us -> 49.7 us
  waiting for transfers between devices: 35.7 us -> 33.1 us
    psum x2 -> x4, blocking collectives: 83 us -> 49.7 us  [the longest x2 25 us: paired_products(): lax.psum((jnp.sum(residual * precond), jnp.sum(precond * image)), 'gz')]
    all_gather x1, waiting for transfers between devices: 17.5 us -> 14.9 us  [local(): slab_pressure = lax.all_gather(solution, 'size', axis=1, tiled=True)]
where the time goes in v1:
time: 194 us; the launch traced here: 193 us
  other arithmetic  50.5 us (26%)
  blocking collectives  49.7 us (26%)
  starting transfers between devices  34 us (18%)
  waiting for transfers between devices  33.1 us (17%)
  between operations  21.7 us (11%)
  local copies, waits for them, and re-layouts  4.25 us (2%)
    psum x2, blocking collectives, paired_products(): lax.psum((jnp.sum(residual * precond), jnp.sum(precond * image)), 'gz')  25 us
    psum x2, blocking collectives, paired_products(): lax.psum(lax.psum((jnp.sum(residual * precond), jnp.sum(precond * image))...  24.7 us
    ppermute x7, starting transfers between devices, extended(): lax.ppermute(tail, axis, [(i, (i + 1) % count) for i in range(ends)])  21.3 us
    ppermute x7, waiting for transfers between devices, extended(): lax.ppermute(tail, axis, [(i, (i + 1) % count) for i in range(ends)])  18 us
    all_gather x1, waiting for transfers between devices, local(): slab_pressure = lax.all_gather(solution, 'size', axis=1, tiled=True)  14.9 us
    ppermute x7, starting transfers between devices, extended(): lax.ppermute(head, axis, [((i + 1) % count, i) for i in range(ends)])  12.7 us
    reduce_sum x2, other arithmetic, paired_products(): jnp.sum(precond * image)  9.75 us
    mul x2, other arithmetic, apply_operator(): scaled = conduct * vector  9.73 us
  transfers between devices with their start and end apart: 15, of which 8 were waited for; matrix products, arithmetic and copies ran while one was open for 3% of the time, Pallas kernels for 0%

profile of v1, /device:TPU:4, one launch (start us, length us, event | category | flops | bytes accessed | tf_op | source)
XLA Modules:
  0.0 193.2 jit_solution(9540197274437170267)
XLA Ops:
  7.2 1.4 fusion.53
  8.6 1.4 fusion.52
  10.1 5.0 %fusion.39 = (f32[32,16,128]{2,1,0:T(8,128)S(1)}, pred[32,16,128]{2,1,0:T(8,128)(4,1)S(1)}, pred[32,16,128]{2,1,0:T(8,128)(4,1)S(1)}) fusion(f32[]{:T(128)} %bitcast.5, f32[]{:T(128)} %bitcast.4, f32[]{:T(128)} %bitcast.3, f32[32,16,128]{2,1,0:T(8,128)} %param.10, f32[]{:T(128)} %bitcast.2, f32[]{:T(128)} %bitcast.1, f32[]{:T(128)} %bitcast, ...), kind=kLoop, calls=%fused_computation.127 | loop fusion | flops 786432 | bytes 917532 | tf_op jit(solution)/shard_map/mul | solution.py:40
  15.1 1.3 collective-permute-start.1
  16.4 4.5 %collective-permute-start = (f32[32,1,128]{2,1,0:T(1,128)S(1)}, f32[32,1,128]{2,1,0:T(1,128)S(1)}, u32[]{:S(2)}, u32[]{:S(2)}) collective-permute-start(f32[32,1,128]{2,1,0:T(1,128)S(1)} %get-tuple-element.45), channel_id=1, source_target_pairs={{0,8},{8,16},{16,24},{1,9},{9,17},{17,25},{2,10},{10,18},{18,26},{... | collective-permute-start | bytes 49160 | tf_op jit(solution)/shard_map/ppermute | solution.py:19
  21.0 1.4 collective-permute-done
  22.4 1.9 collective-permute-start.2
  24.4 2.4 %collective-permute-start.3 = (f32[1,18,128]{2,1,0:T(8,128)S(1)}, f32[1,18,128]{2,1,0:T(8,128)S(1)}, u32[]{:S(2)}, u32[]{:S(2)}) collective-permute-start(f32[1,18,128]{2,1,0:T(8,128)S(1)} %get-tuple-element.41), channel_id=1, source_target_pairs={{0,1},{1,2},{2,3},{3,4},{4,5},{5,6},{6,7},{8,9},{9,10},{10,11},{11... | collective-permute-start | bytes 27656 | tf_op jit(solution)/shard_map/ppermute | solution.py:19
  26.8 3.5 %collective-permute-done.3 = f32[1,18,128]{2,1,0:T(8,128)S(1)} collective-permute-done((f32[1,18,128]{2,1,0:T(8,128)S(1)}, f32[1,18,128]{2,1,0:T(8,128)S(1)}, u32[]{:S(2)}, u32[]{:S(2)}) %collective-permute-start.3) | collective-permute-done | bytes 9248 | tf_op jit(solution)/shard_map/ppermute | solution.py:19
  30.7 4.9 %multiply_reduce_fusion.1 = (f32[]{:T(128)}, f32[]{:T(128)}, f32[32,16,128]{2,1,0:T(8,128)S(1)}) fusion(pred[32,16,128]{2,1,0:T(8,128)(4,1)S(1)} %get-tuple-element.27, pred[32,16,128]{2,1,0:T(8,128)(4,1)S(1)} %get-tuple-element.26, f32[]{:T(128)} %bitcast.5, f32[]{:T(128)} %bitcast.4, f32[]{:T(128)} %bitcast.3, f32[32,16,128]{2,1,0:T(8,128)S(1)} %copy-done.1, ...), kind=kLoop, calls=%fused_computation.123 | loop fusion | flops 2031614 | bytes 1493024 | tf_op jit(solution)/shard_map/reduce_sum | solution.py:47
  35.6 12.5 %all-reduce.6 = (f32[]{:T(128)}, f32[]{:T(128)}) all-reduce(f32[]{:T(128)} %get-tuple-element.4, f32[]{:T(128)} %get-tuple-element.3), channel_id=1, replica_groups=mesh['size'=4,'gz'=8] {'gz'}, use_global_device_ids=true, to_apply=%region_1.2 | all-reduce | flops 2 | bytes 16 | tf_op jit(solution)/shard_map/psum | solution.py:47
  48.1 13.3 %all-reduce.8 = (f32[]{:T(128)}, f32[]{:T(128)}) all-reduce(f32[]{:T(128)} %get-tuple-element.7, f32[]{:T(128)} %get-tuple-element.8), channel_id=1, replica_groups=mesh['size'=4,'gz'=8] {'size'}, use_global_device_ids=true, to_apply=%region_2.3 | all-reduce | flops 2 | bytes 16 | tf_op jit(solution)/shard_map/psum | solution.py:47
  62.8 4.7 %fusion.38 = (f32[32,16,128]{2,1,0:T(8,128)S(1)}, f32[]{:T(128)}) fusion(pred[32,16,128]{2,1,0:T(8,128)(4,1)S(1)} %get-tuple-element.27, pred[32,16,128]{2,1,0:T(8,128)(4,1)S(1)} %get-tuple-element.26, f32[]{:T(128)} %bitcast.5, f32[]{:T(128)} %bitcast.4, f32[]{:T(128)} %bitcast.3, f32[32,16,128]{2,1,0:T(8,128)S(1)} %get-tuple-element.24, f32[]{:T(128)S(6)} %div.19, ...), kind=kLoop, calls=%fused_computation.126 | loop fusion | flops 917503 | bytes 917536 | tf_op jit(solution)/shard_map/mul | solution.py:40
  67.5 1.3 collective-permute-start.5
  68.8 4.7 %collective-permute-start.4 = (f32[32,1,128]{2,1,0:T(1,128)S(1)}, f32[32,1,128]{2,1,0:T(1,128)S(1)}, u32[]{:S(2)}, u32[]{:S(2)}) collective-permute-start(f32[32,1,128]{2,1,0:T(1,128)S(1)} %get-tuple-element.43), channel_id=1, source_target_pairs={{0,8},{8,16},{16,24},{1,9},{9,17},{17,25},{2,10},{10,18},{18,26},{... | collective-permute-start | bytes 49160 | tf_op jit(solution)/shard_map/ppermute | solution.py:19
  73.5 1.4 collective-permute-done.4
  74.9 1.9 collective-permute-start.6
  76.8 2.4 %collective-permute-start.7 = (f32[1,18,128]{2,1,0:T(8,128)S(1)}, f32[1,18,128]{2,1,0:T(8,128)S(1)}, u32[]{:S(2)}, u32[]{:S(2)}) collective-permute-start(f32[1,18,128]{2,1,0:T(8,128)S(1)} %get-tuple-element.39), channel_id=1, source_target_pairs={{0,1},{1,2},{2,3},{3,4},{4,5},{5,6},{6,7},{8,9},{9,10},{10,11},{11... | collective-permute-start | bytes 27656 | tf_op jit(solution)/shard_map/ppermute | solution.py:19
  79.3 3.5 %collective-permute-done.7 = f32[1,18,128]{2,1,0:T(8,128)S(1)} collective-permute-done((f32[1,18,128]{2,1,0:T(8,128)S(1)}, f32[1,18,128]{2,1,0:T(8,128)S(1)}, u32[]{:S(2)}, u32[]{:S(2)}) %collective-permute-start.7) | collective-permute-done | bytes 9248 | tf_op jit(solution)/shard_map/ppermute | solution.py:19
  82.8 0.4 select_maximum_fusion.8
  83.2 4.9 %fusion.28 = f32[]{:T(128)} fusion(f32[34,18,130]{2,1,0:T(8,128)S(1)} %select_maximum_fusion.8, f32[32,16,128]{2,1,0:T(8,128)S(1)} %get-tuple-element.37, f32[32,1,128]{2,1,0:T(1,128)S(1)} %collective-permute-done.4, f32[32,1,128]{2,1,0:T(1,128)S(1)} %collective-permute-done.5, f32[1,18,128]{2,1,0:T(8,128)S(1)} %collective-permute-done.7, ...), kind=kLoop, calls=%fused_computation.91 | loop fusion | flops 2031615 | bytes 1493024 | tf_op jit(solution)/shard_map/reduce_sum | solution.py:47
  88.1 12.5 %all-reduce.5 = (f32[]{:T(128)}, f32[]{:T(128)}) all-reduce(f32[]{:T(128)} %get-tuple-element.38, f32[]{:T(128)} %fusion.28), channel_id=1, replica_groups=mesh['size'=4,'gz'=8] {'gz'}, use_global_device_ids=true, to_apply=%region_7.8 | all-reduce | flops 2 | bytes 16 | tf_op jit(solution)/shard_map/psum | solution.py:47
  100.6 11.4 %all-reduce.7 = (f32[]{:T(128)}, f32[]{:T(128)}) all-reduce(f32[]{:T(128)} %get-tuple-element.5, f32[]{:T(128)} %get-tuple-element.6), channel_id=1, replica_groups=mesh['size'=4,'gz'=8] {'size'}, use_global_device_ids=true, to_apply=%region_8.9 | all-reduce | flops 2 | bytes 16 | tf_op jit(solution)/shard_map/psum | solution.py:47
  116.6 4.7 %multiply_add_fusion.6 = f32[32,16,128]{2,1,0:T(8,128)} fusion(f32[]{:T(128)S(6)} %div.21, f32[]{:T(128)S(6)} %div.23, f32[]{:T(128)S(6)} %div.19, pred[32,16,128]{2,1,0:T(8,128)(4,1)S(1)} %get-tuple-element.27, pred[32,16,128]{2,1,0:T(8,128)(4,1)S(1)} %get-tuple-element.26, f32[]{:T(128)} %bitcast.5, f32[]{:T(128)} %bitcast.4, f32[]{:T(128)} %bitcast.3, ...), kind=kLoop, calls=%fused_computation.120 | loop fusion | flops 1114112 | bytes 917540 | tf_op jit(solution)/shard_map/add | solution.py:120
  121.4 1.9 collective-permute-start.11
  123.3 2.4 %collective-permute-start.10 = (f32[1,64,128]{2,1,0:T(8,128)S(1)}, f32[1,64,128]{2,1,0:T(8,128)S(1)}, u32[]{:S(2)}, u32[]{:S(2)}) collective-permute-start(f32[1,64,128]{2,1,0:T(8,128)S(1)} %get-tuple-element.35), channel_id=1, source_target_pairs={{0,1},{1,2},{2,3},{3,4},{4,5},{5,6},{6,7},{8,9},{9,10},{10,11},{11... | collective-permute-start | bytes 98312 | tf_op jit(solution)/shard_map/ppermute | solution.py:19
  127.0 0.6 fusion.51
  127.6 2.3 %select_bitcast_fusion.1 = (f32[1,32,64,128]{3,2,1,0:T(8,128)S(1)}, pred[32,64,128]{2,1,0:T(8,128)(4,1)S(1)}, pred[32,64,128]{2,1,0:T(8,128)(4,1)S(1)}) fusion(f32[]{:T(128)} %bitcast.5, f32[]{:T(128)} %bitcast.4, f32[]{:T(128)} %bitcast.3, s32[32,64,128]{2,1,0:T(8,128)S(1)} %copy-done.3), kind=kLoop, calls=%fused_computation.70 | loop fusion | flops 1048576 | bytes 2621452 | tf_op jit(solution)/shard_map/stack | solution.py:134
  129.9 1.9 select_bitcast_fusion
  131.8 14.9 %all-gather.2.cloned.1.call-done = f32[32,64,128]{2,1,0:T(8,128)} async-done(((f32[32,16,128]{2,1,0:T(8,128)}), f32[32,64,128]{2,1,0:T(8,128)}) %all-gather.2.cloned.1.call-update) | async-done | bytes 1048592 | tf_op jit(solution)/shard_map/all_gather | solution.py:133
  146.7 0.9 pad_maximum_fusion.22
  147.6 2.5 %collective-permute-start.9 = (f32[3,2,64,128]{3,2,1,0:T(8,128)S(1)}, f32[3,2,64,128]{3,2,1,0:T(8,128)S(1)}, u32[]{:S(2)}, u32[]{:S(2)}) collective-permute-start(f32[3,2,64,128]{3,2,1,0:T(8,128)S(1)} %get-tuple-element.32), channel_id=1, source_target_pairs={{1,0},{2,1},{3,2},{4,3},{5,4},{6,5},{7,6},{9,8},{10,9},{11,10},{12... | collective-permute-start | bytes 589832 | tf_op jit(solution)/shard_map/ppermute | solution.py:21
  150.1 2.2 %collective-permute-start.8 = (f32[3,2,64,128]{3,2,1,0:T(8,128)S(1)}, f32[3,2,64,128]{3,2,1,0:T(8,128)S(1)}, u32[]{:S(2)}, u32[]{:S(2)}) collective-permute-start(f32[3,2,64,128]{3,2,1,0:T(8,128)S(1)} %get-tuple-element.31), channel_id=1, source_target_pairs={{0,1},{1,2},{2,3},{3,4},{4,5},{5,6},{6,7},{8,9},{9,10},{10,11},{11... | collective-permute-start | bytes 589832 | tf_op jit(solution)/shard_map/ppermute | solution.py:19
  152.3 0.7 select_maximum_fusion.6
  153.3 4.7 %collective-permute-done.8 = f32[3,2,64,128]{3,2,1,0:T(8,128)S(1)} collective-permute-done((f32[3,2,64,128]{3,2,1,0:T(8,128)S(1)}, f32[3,2,64,128]{3,2,1,0:T(8,128)S(1)}, u32[]{:S(2)}, u32[]{:S(2)}) %collective-permute-start.8) | collective-permute-done | bytes 196640 | tf_op jit(solution)/shard_map/ppermute | solution.py:19
  158.0 7.3 %select_maximum_fusion = f32[3,36,66,130]{3,2,1,0:T(8,128)S(1)} fusion(f32[3,2,64,128]{3,2,1,0:T(8,128)S(1)} %collective-permute-done.9, f32[3,2,64,128]{3,2,1,0:T(8,128)S(1)} %collective-permute-done.8, f32[1,32,64,128]{3,2,1,0:T(8,128)S(1)} %select_bitcast_fusion, f32[1,32,64,128]{3,2,1,0:T(8,128)S(1)} %get-tuple-element.21, f32[1,32,64,128]{3,2,1,0:T(8,128)S(1)} %bitcast.52), kind=kLoop, calls=%fused_computation.4 | loop fusion | flops 19459440 | bytes 7245504 | tf_op jit(solution)/shard_map/concatenate | solution.py:17
  165.3 0.7 slice_bitcast_fusion.2
  165.9 2.4 %multiply_add_fusion.1 = (f32[32,64,129]{2,1,0:T(8,128)S(1)}, f32[32,64,129]{2,1,0:T(8,128)S(1)}) fusion(f32[34,66,130]{2,1,0:T(8,128)S(1)} %select_maximum_fusion.6, f32[]{:T(128)} %bitcast.45, f32[34,66,130]{2,1,0:T(8,128)S(1)} %get-tuple-element.29, f32[34,66,130]{2,1,0:T(8,128)S(1)} %get-tuple-element.28, f32[]{:T(128)} %bitcast.42), kind=kLoop, calls=%fused_computation.30 | loop fusion | flops 3170304 | bytes 8454152 | tf_op jit(solution)/shard_map/add | solution.py:77
  168.3 1.9 multiply_add_fusion.3
  170.3 1.2 multiply_add_fusion.5
  171.5 2.1 %fusion.21 = (f32[1,32,64,128]{3,2,1,0:T(8,128)}, f32[32,64,128]{2,1,0:T(8,128)S(1)}) fusion(f32[1,32,64,128]{3,2,1,0:T(8,128)S(1)} %copy-done.4, f32[34,66,130]{2,1,0:T(8,128)S(1)} %get-tuple-element.30, f32[1,32,64,128]{3,2,1,0:T(8,128)S(1)} %copy-done, f32[32,64,129]{2,1,0:T(8,128)S(1)} %get-tuple-element.19, f32[32,65,128]{2,1,0:T(8,128)S(1)} %get-tuple-element.17, ...), kind=kLoop, calls=%fused_computation.68 | loop fusion | flops 3670016 | bytes 11534336 | tf_op jit(solution)/shard_map/broadcast_in_dim | solution.py:146
  173.6 1.9 collective-permute-start.13
  175.5 2.6 %collective-permute-start.12 = (f32[1,64,128]{2,1,0:T(8,128)S(1)}, f32[1,64,128]{2,1,0:T(8,128)S(1)}, u32[]{:S(2)}, u32[]{:S(2)}) collective-permute-start(f32[1,64,128]{2,1,0:T(8,128)S(1)} %get-tuple-element.33), channel_id=1, source_target_pairs={{0,1},{1,2},{2,3},{3,4},{4,5},{5,6},{6,7},{8,9},{9,10},{10,11},{11... | collective-permute-start | bytes 98312 | tf_op jit(solution)/shard_map/ppermute | solution.py:19
  178.1 3.5 %collective-permute-done.12 = f32[1,64,128]{2,1,0:T(8,128)S(1)} collective-permute-done((f32[1,64,128]{2,1,0:T(8,128)S(1)}, f32[1,64,128]{2,1,0:T(8,128)S(1)}, u32[]{:S(2)}, u32[]{:S(2)}) %collective-permute-start.12) | collective-permute-done | bytes 32800 | tf_op jit(solution)/shard_map/ppermute | solution.py:19
  181.6 0.7 select_maximum_fusion.4
  182.3 1.2 multiply_add_fusion
  183.5 0.7 multiply_add_fusion.2
  184.5 1.9 fusion.13
  (38 shorter events, 1.1 us)
Async XLA Ops:
  7.2 23.5 %copy-start.1 = (f32[32,16,128]{2,1,0:T(8,128)S(1)}, f32[32,16,128]{2,1,0:T(8,128)}, u32[]{:S(2)}) copy-start(f32[32,16,128]{2,1,0:T(8,128)} %param.10) | copy-start | bytes 786436
  7.2 139.5 %all-gather.2.cloned.1.call-start = ((), (), s32[]{:S(2)}) async-start(), calls=%async_computation | async-start | bytes 1310720 | tf_op jit(solution)/shard_map/all_gather | solution.py:133
  15.1 5.9 %collective-permute-start.1 = (f32[32,1,128]{2,1,0:T(1,128)S(1)}, f32[32,1,128]{2,1,0:T(1,128)S(1)}, u32[]{:S(2)}, u32[]{:S(2)}) collective-permute-start(f32[32,1,128]{2,1,0:T(1,128)S(1)} %get-tuple-element.46), channel_id=1, source_target_pairs={{8,0},{16,8},{24,16},{9,1},{17,9},{25,17},{10,2},{18,10},{26,18},{... | collective-permute-start | bytes 49160 | tf_op jit(solution)/shard_map/ppermute | solution.py:21
  16.4 6.0 %collective-permute-start = (f32[32,1,128]{2,1,0:T(1,128)S(1)}, f32[32,1,128]{2,1,0:T(1,128)S(1)}, u32[]{:S(2)}, u32[]{:S(2)}) collective-permute-start(f32[32,1,128]{2,1,0:T(1,128)S(1)} %get-tuple-element.45), channel_id=1, source_target_pairs={{0,8},{8,16},{16,24},{1,9},{9,17},{17,25},{2,10},{10,18},{18,26},{... | collective-permute-start | bytes 49160 | tf_op jit(solution)/shard_map/ppermute | solution.py:19
  22.4 4.3 %collective-permute-start.2 = (f32[1,18,128]{2,1,0:T(8,128)S(1)}, f32[1,18,128]{2,1,0:T(8,128)S(1)}, u32[]{:S(2)}, u32[]{:S(2)}) collective-permute-start(f32[1,18,128]{2,1,0:T(8,128)S(1)} %get-tuple-element.42), channel_id=1, source_target_pairs={{1,0},{2,1},{3,2},{4,3},{5,4},{6,5},{7,6},{9,8},{10,9},{11,10},{12... | collective-permute-start | bytes 27656 | tf_op jit(solution)/shard_map/ppermute | solution.py:21
  24.4 5.9 %collective-permute-start.3 = (f32[1,18,128]{2,1,0:T(8,128)S(1)}, f32[1,18,128]{2,1,0:T(8,128)S(1)}, u32[]{:S(2)}, u32[]{:S(2)}) collective-permute-start(f32[1,18,128]{2,1,0:T(8,128)S(1)} %get-tuple-element.41), channel_id=1, source_target_pairs={{0,1},{1,2},{2,3},{3,4},{4,5},{5,6},{6,7},{8,9},{9,10},{10,11},{11... | collective-permute-start | bytes 27656 | tf_op jit(solution)/shard_map/ppermute | solution.py:19
  67.5 6.0 %collective-permute-start.5 = (f32[32,1,128]{2,1,0:T(1,128)S(1)}, f32[32,1,128]{2,1,0:T(1,128)S(1)}, u32[]{:S(2)}, u32[]{:S(2)}) collective-permute-start(f32[32,1,128]{2,1,0:T(1,128)S(1)} %get-tuple-element.44), channel_id=1, source_target_pairs={{8,0},{16,8},{24,16},{9,1},{17,9},{25,17},{10,2},{18,10},{26,18},{... | collective-permute-start | bytes 49160 | tf_op jit(solution)/shard_map/ppermute | solution.py:21
  68.8 52.6 %copy-start = (f32[1,32,64,128]{3,2,1,0:T(8,128)S(1)}, f32[1,32,64,128]{3,2,1,0:T(8,128)}, u32[]{:S(2)}) copy-start(f32[1,32,64,128]{3,2,1,0:T(8,128)} %param.16) | copy-start | bytes 3145732
  68.8 58.2 %copy-start.9 = (f32[1,3]{1,0:T(1,128)S(1)}, f32[1,3]{1,0:T(1,128)}, u32[]{:S(2)}) copy-start(f32[1,3]{1,0:T(1,128)} %param.13) | copy-start | bytes 40
  68.8 58.8 %copy-start.3 = (s32[32,64,128]{2,1,0:T(8,128)S(1)}, s32[32,64,128]{2,1,0:T(8,128)}, u32[]{:S(2)}) copy-start(s32[32,64,128]{2,1,0:T(8,128)} %param.9) | copy-start | bytes 3145732
  68.8 6.1 %collective-permute-start.4 = (f32[32,1,128]{2,1,0:T(1,128)S(1)}, f32[32,1,128]{2,1,0:T(1,128)S(1)}, u32[]{:S(2)}, u32[]{:S(2)}) collective-permute-start(f32[32,1,128]{2,1,0:T(1,128)S(1)} %get-tuple-element.43), channel_id=1, source_target_pairs={{0,8},{8,16},{16,24},{1,9},{9,17},{17,25},{2,10},{10,18},{18,26},{... | collective-permute-start | bytes 49160 | tf_op jit(solution)/shard_map/ppermute | solution.py:19
  74.9 4.3 %collective-permute-start.6 = (f32[1,18,128]{2,1,0:T(8,128)S(1)}, f32[1,18,128]{2,1,0:T(8,128)S(1)}, u32[]{:S(2)}, u32[]{:S(2)}) collective-permute-start(f32[1,18,128]{2,1,0:T(8,128)S(1)} %get-tuple-element.40), channel_id=1, source_target_pairs={{1,0},{2,1},{3,2},{4,3},{5,4},{6,5},{7,6},{9,8},{10,9},{11,10},{12... | collective-permute-start | bytes 27656 | tf_op jit(solution)/shard_map/ppermute | solution.py:21
  76.8 5.9 %collective-permute-start.7 = (f32[1,18,128]{2,1,0:T(8,128)S(1)}, f32[1,18,128]{2,1,0:T(8,128)S(1)}, u32[]{:S(2)}, u32[]{:S(2)}) collective-permute-start(f32[1,18,128]{2,1,0:T(8,128)S(1)} %get-tuple-element.39), channel_id=1, source_target_pairs={{0,1},{1,2},{2,3},{3,4},{4,5},{5,6},{6,7},{8,9},{9,10},{10,11},{11... | collective-permute-start | bytes 27656 | tf_op jit(solution)/shard_map/ppermute | solution.py:19
  121.4 30.9 %collective-permute-start.11 = (f32[1,64,128]{2,1,0:T(8,128)S(1)}, f32[1,64,128]{2,1,0:T(8,128)S(1)}, u32[]{:S(2)}, u32[]{:S(2)}) collective-permute-start(f32[1,64,128]{2,1,0:T(8,128)S(1)} %get-tuple-element.36), channel_id=1, source_target_pairs={{1,0},{2,1},{3,2},{4,3},{5,4},{6,5},{7,6},{9,8},{10,9},{11,10},{12... | collective-permute-start | bytes 98312 | tf_op jit(solution)/shard_map/ppermute | solution.py:21
  123.3 29.0 %collective-permute-start.10 = (f32[1,64,128]{2,1,0:T(8,128)S(1)}, f32[1,64,128]{2,1,0:T(8,128)S(1)}, u32[]{:S(2)}, u32[]{:S(2)}) collective-permute-start(f32[1,64,128]{2,1,0:T(8,128)S(1)} %get-tuple-element.35), channel_id=1, source_target_pairs={{0,1},{1,2},{2,3},{3,4},{4,5},{5,6},{6,7},{8,9},{9,10},{10,11},{11... | collective-permute-start | bytes 98312 | tf_op jit(solution)/shard_map/ppermute | solution.py:19
  147.6 10.4 %copy-start.2 = (f32[32,64,128]{2,1,0:T(8,128)S(1)}, f32[32,64,128]{2,1,0:T(8,128)}, u32[]{:S(2)}) copy-start(f32[32,64,128]{2,1,0:T(8,128)} %all-gather.2.cloned.1.call-done) | copy-start | bytes 3145732
  147.6 5.6 %collective-permute-start.9 = (f32[3,2,64,128]{3,2,1,0:T(8,128)S(1)}, f32[3,2,64,128]{3,2,1,0:T(8,128)S(1)}, u32[]{:S(2)}, u32[]{:S(2)}) collective-permute-start(f32[3,2,64,128]{3,2,1,0:T(8,128)S(1)} %get-tuple-element.32), channel_id=1, source_target_pairs={{1,0},{2,1},{3,2},{4,3},{5,4},{6,5},{7,6},{9,8},{10,9},{11,10},{12... | collective-permute-start | bytes 589832 | tf_op jit(solution)/shard_map/ppermute | solution.py:21
  150.1 7.9 %collective-permute-start.8 = (f32[3,2,64,128]{3,2,1,0:T(8,128)S(1)}, f32[3,2,64,128]{3,2,1,0:T(8,128)S(1)}, u32[]{:S(2)}, u32[]{:S(2)}) collective-permute-start(f32[3,2,64,128]{3,2,1,0:T(8,128)S(1)} %get-tuple-element.31), channel_id=1, source_target_pairs={{0,1},{1,2},{2,3},{3,4},{4,5},{5,6},{6,7},{8,9},{9,10},{10,11},{11... | collective-permute-start | bytes 589832 | tf_op jit(solution)/shard_map/ppermute | solution.py:19
  152.3 5.7 %copy-start.5 = (f32[1,64,128]{2,1,0:T(8,128)}, f32[1,64,128]{2,1,0:T(8,128)S(1)}, u32[]{:S(2)}) copy-start(f32[1,64,128]{2,1,0:T(8,128)S(1)} %collective-permute-done.11) | copy-start | bytes 98308
  152.3 5.7 %copy-start.7 = (f32[1,64,128]{2,1,0:T(8,128)}, f32[1,64,128]{2,1,0:T(8,128)S(1)}, u32[]{:S(2)}) copy-start(f32[1,64,128]{2,1,0:T(8,128)S(1)} %collective-permute-done.10) | copy-start | bytes 98308
  168.3 1.9 copy-start.6
  168.3 1.9 copy-start.8
  170.3 1.2 copy-start.4
  173.6 4.6 %collective-permute-start.13 = (f32[1,64,128]{2,1,0:T(8,128)S(1)}, f32[1,64,128]{2,1,0:T(8,128)S(1)}, u32[]{:S(2)}, u32[]{:S(2)}) collective-permute-start(f32[1,64,128]{2,1,0:T(8,128)S(1)} %get-tuple-element.34), channel_id=1, source_target_pairs={{1,0},{2,1},{3,2},{4,3},{5,4},{6,5},{7,6},{9,8},{10,9},{11,10},{12... | collective-permute-start | bytes 98312 | tf_op jit(solution)/shard_map/ppermute | solution.py:21
  175.5 6.1 %collective-permute-start.12 = (f32[1,64,128]{2,1,0:T(8,128)S(1)}, f32[1,64,128]{2,1,0:T(8,128)S(1)}, u32[]{:S(2)}, u32[]{:S(2)}) collective-permute-start(f32[1,64,128]{2,1,0:T(8,128)S(1)} %get-tuple-element.33), channel_id=1, source_target_pairs={{0,1},{1,2},{2,3},{3,4},{4,5},{5,6},{6,7},{8,9},{9,10},{10,11},{11... | collective-permute-start | bytes 98312 | tf_op jit(solution)/shard_map/ppermute | solution.py:19
Sparse Core Ops, SparseCore 0:
  121.5 25.2 all-gather.1
